TPU v7x, 128 devices: a whole 4x4x4 slice. The times are simulated.
128 devices in a mesh: row: 8 (over y, core), col: 16 (over x, z).
Axes of the slice: x: 4, y: 4, z: 4, core: 2. Of those that a mesh axis runs over, the one named last changes fastest.
Arguments:
- theta: float32 [64, 256, 256], P('row', None, 'col'), may hold values from -6 to 6
- left_env: float32 [32, 32, 256, 256], P('row', 'col'), as said below
- right_env: float32 [8, 32, 256, 256], P(None, 'col'), as said below
- left_sector: int32 [64], replicated, may hold values from 0 to 31, as said below
- right_sector: int32 [64], P('row'), may hold values from 0 to 7
- term_on: int32 [64, 32], P('row', 'col'), may hold values 0 or 1
- left_size: int32 [32], replicated, may hold values from 1 to 256, 5120 in all
- right_size: int32 [8], replicated, may hold values from 1 to 256, 1280 in all
Outputs:
- new_theta: float32 [64, 256, 256], P('row', None, 'col')
- energy: float32 [], replicated
Inputs may be any that keep to these rules, and one draw needn't show every extreme that they name: `left_sector`: left sector s belongs to row s // 4. Block k belongs to row k // 8. The 8 blocks of one row name distinct left sectors; they name either none or exactly 2 sectors belonging to any one row, and the blocks of every row name 2 sectors belonging to one common row. `left_env`: each tile is symmetric in its last two dimensions. `right_env`: each tile is symmetric in its last two dimensions.
All inputs are finite; a program needn't handle non-finite values. No bound on the sum of `term_on` on one device may be relied on, other than what follows from the above.
Results may differ from a plain program's by a relative error of at most 0.0001.
Values sent between devices are 32-bit elements; how exact they have to be, the bound alone decides.
No kernel may reach another device: no remote copies, remote signals or barrier semaphores. Data moves between devices by JAX's collectives and lax.ppermute only.
A program may use at most 128 MiB of HBM per device.

v0:
```python
import jax
import jax.numpy as jnp
from jax import lax
from jax.sharding import PartitionSpec as P

ITERS = 2
highest = lax.Precision.HIGHEST


def lookup(small_table, index_list):
    slot_hits = index_list[:, None] == jnp.arange(small_table.shape[0], dtype=jnp.int32)[None, :]
    return jnp.sum(jnp.where(slot_hits, small_table[None, :], 0), axis=1)


def tile_masks(left_ids, right_ids, left_size, right_size, tile_size, offset, span_cols):
    rows_live = lookup(left_size, left_ids)
    cols_live = lookup(right_size, right_ids)
    row_mask = (jnp.arange(tile_size, dtype=jnp.int32)[None, :] < rows_live[:, None]).astype(
        jnp.float32
    )
    col_mask = (
        (offset + jnp.arange(span_cols, dtype=jnp.int32))[None, :] < cols_live[:, None]
    ).astype(jnp.float32)
    return row_mask[:, :, None] * col_mask[:, None, :]


def local(theta, left_env, right_env, left_sector, right_sector, term_on, left_size, right_size):
    row_count = lax.axis_size("row")
    blocks, tile_size, thin_cols = theta.shape
    local_sectors = left_env.shape[0]
    capacity = max(2, 2 * blocks // row_count)
    row_index = lax.axis_index("row")
    col_index = lax.axis_index("col")
    own_left = lax.dynamic_slice_in_dim(left_sector, row_index * blocks, blocks)
    offset = col_index * thin_cols
    span_cols = theta.shape[2]
    start_mask = tile_masks(
        own_left, right_sector, left_size, right_size, tile_size, offset, span_cols
    )
    start_vec = theta * start_mask
    senders = row_index * local_sectors + jnp.arange(local_sectors, dtype=jnp.int32)
    wanted = left_sector.reshape(row_count, blocks)
    used_flag = jnp.any(wanted[:, :, None] == senders[None, None, :], axis=1)
    used_count = used_flag.astype(jnp.int32)
    before = jnp.cumsum(used_count, axis=1) - used_count
    pick_flag = used_flag[:, None, :] & (
        before[:, None, :] == jnp.arange(capacity, dtype=jnp.int32)[None, :, None]
    )
    filled = jnp.any(pick_flag, axis=2).reshape(-1)
    local_index = jnp.sum(
        jnp.where(pick_flag, jnp.arange(local_sectors, dtype=jnp.int32)[None, None, :], 0), axis=2
    ).reshape(-1)
    outgoing = (
        jnp.take(left_env, local_index, axis=0) * filled.astype(jnp.float32)[:, None, None, None]
    )
    arrived = lax.all_to_all(outgoing, "row", split_axis=0, concat_axis=0, tiled=True)
    every_sector = jnp.arange(row_count * local_sectors, dtype=jnp.int32)
    needed = (
        jnp.any(own_left[:, None] == every_sector[None, :], axis=0)
        .astype(jnp.int32)
        .reshape(row_count, local_sectors)
    )
    order_rank = (jnp.cumsum(needed, axis=1) - needed).reshape(-1)
    position = own_left // local_sectors * capacity + lookup(order_rank, own_left)
    left_pick = jnp.take(arrived, position, axis=0)
    right_pick = jnp.take(right_env, right_sector, axis=0)
    weights = term_on.astype(jnp.float32)

    def contract(full_vector):
        middle = (
            jnp.einsum("swia,sab->swib", left_pick, full_vector, precision=highest)
            * weights[:, :, None, None]
        )
        return jnp.einsum("swib,swjb->sij", middle, right_pick, precision=highest)

    def operate(vector):
        full_vector = lax.all_gather(vector, "col", axis=2, tiled=True)
        total_sum = lax.psum_scatter(contract(full_vector), "col", scatter_dimension=2, tiled=True)
        return total_sum * start_mask

    def combine(values):
        reduced = lax.psum(values, ("row", "col"))
        return reduced

    image_vec = operate(start_vec)
    norm_sq, correlation = combine((jnp.sum(start_vec * start_vec), jnp.sum(start_vec * image_vec)))
    inv_norm = 1.0 / jnp.sqrt(norm_sq)
    basis_vec = start_vec * inv_norm
    applied = image_vec * inv_norm
    ritz_value = correlation / norm_sq
    for turn_index in range(ITERS):
        residual = applied - ritz_value * basis_vec
        (res_sq,) = combine((jnp.sum(residual * residual),))
        length = jnp.sqrt(res_sq)
        fresh_vec = residual / length
        fresh_applied = operate(fresh_vec)
        (curvature,) = combine((jnp.sum(fresh_vec * fresh_applied),))
        half_gap = 0.5 * (ritz_value - curvature)
        root_term = jnp.sqrt(half_gap * half_gap + res_sq)
        lowest = 0.5 * (ritz_value + curvature) - root_term
        first_coef = curvature - lowest
        pair_norm = jnp.sqrt(first_coef * first_coef + res_sq)
        basis_vec = (first_coef * basis_vec - length * fresh_vec) / pair_norm
        applied = (first_coef * applied - length * fresh_applied) / pair_norm
        ritz_value = lowest
    total_entries = blocks * row_count * tile_size * tile_size
    output = basis_vec * jnp.sqrt(jnp.float32(total_entries))
    return (output, ritz_value)


def solution(mesh):
    placed = (
        P("row", None, "col"),
        P("row", "col", None, None),
        P(None, "col", None, None),
        P(),
        P("row"),
        P("row", "col"),
        P(),
        P(),
    )
    return jax.shard_map(
        local, mesh=mesh, in_specs=placed, out_specs=(P("row", None, "col"), P()), check_vma=False
    )
```

profile of v0, /device:TPU:1, one launch (start us, length us, event | category | flops | bytes accessed | tf_op | source)
XLA Modules:
  0.0 820.7 jit_solution(7117098073512323360)
XLA Ops:
  7.2 0.9 eq.29
  8.1 0.2 compare_reduce_fusion
  8.4 0.1 copy.12
  8.5 0.1 reshape.147
  8.5 0.1 reshape.146
  8.7 0.1 copy.14
  8.8 0.1 reshape.149
  8.9 4.3 gather_fusion
  13.2 7.9 select_multiply_fusion
  21.1 6.4 all-to-all-start
  27.5 0.1 dynamic_slice.3
  27.6 0.1 fusion.51
  27.7 0.1 reshape.148
  27.8 0.2 reduce_window_sum.19
  27.9 0.1 reduce_window_sum.20
  28.0 0.2 select_reduce_fusion
  28.2 0.2 select_reduce_fusion.1
  28.6 0.7 multiply_multiply_fusion.3
  29.4 0.1 copy.15
  29.5 4.9 gather_fusion.2
  34.4 0.1 compare_and_fusion.2
  34.5 86.8 %all-to-all-done = f32[16,2,256,256]{3,2,1,0:T(8,128)} async-done(((f32[16,2,256,256]{3,2,1,0:T(8,128)}), f32[16,2,256,256]{3,2,1,0:T(8,128)}, u32[]{:S(2)}, u32[]{:S(2)}) %all-to-all-start) | async-done | bytes 8388640 | tf_op jit(solution)/shard_map/all_to_all | solution.py:56
  121.4 6.2 gather_fusion.1
  127.6 6.8 fusion.13
  134.4 5.9 fusion.33
  140.3 73.6 %reduce-scatter.4.cloned.1.call-done = f32[8,256,16]{1,2,0:T(8,128)} async-done(((f32[8,256,256]{1,2,0:T(8,128)}), f32[8,256,16]{1,2,0:T(8,128)}) %reduce-scatter.4.cloned.1.call-update) | async-done | bytes 131088 | tf_op jit(solution)/shard_map/reduce_scatter | solution.py:78
  213.9 1.6 multiply_reduce_fusion.4
  215.6 65.9 %all-reduce = (f32[]{:T(128)}, f32[]{:T(128)}) all-reduce(f32[]{:T(128)} %get-tuple-element.3, f32[]{:T(128)} %get-tuple-element.2), channel_id=1, replica_groups=mesh['row'=8,'col'=16] {'row','col'}, use_global_device_ids=true, to_apply=%region_13.14 | all-reduce | flops 2 | bytes 16 | tf_op jit(solution)/shard_map/psum | solution.py:82
  283.5 1.6 multiply_reduce_fusion.2
  285.1 62.7 %psum.44 = f32[]{:T(128)} all-reduce(f32[]{:T(128)} %multiply_reduce_fusion.2), channel_id=1, replica_groups=mesh['row'=8,'col'=16] {'row','col'}, use_global_device_ids=true, to_apply=%region_15.16 | all-reduce | flops 1 | bytes 8 | tf_op jit(solution)/shard_map/psum | solution.py:82
  348.5 1.7 broadcast_divide_fusion.1
  350.2 41.4 %all-gather.6.cloned.1.call-done = f32[8,256,256]{1,2,0:T(8,128)} async-done(((f32[8,256,16]{1,2,0:T(8,128)}), f32[8,256,256]{1,2,0:T(8,128)}) %all-gather.6.cloned.1.call-update) | async-done | bytes 2097168 | tf_op jit(solution)/shard_map/all_gather | solution.py:77
  391.6 6.8 fusion.11
  398.5 5.9 fusion.38
  404.4 73.2 %reduce-scatter.6.cloned.1.call-done = f32[8,256,16]{1,2,0:T(8,128)} async-done(((f32[8,256,256]{1,2,0:T(8,128)}), f32[8,256,16]{1,2,0:T(8,128)}) %reduce-scatter.6.cloned.1.call-update) | async-done | bytes 131088 | tf_op jit(solution)/shard_map/reduce_scatter | solution.py:78
  477.6 1.6 multiply_reduce_fusion.1
  479.2 65.8 %psum.45 = f32[]{:T(128)} all-reduce(f32[]{:T(128)} %multiply_reduce_fusion.1), channel_id=1, replica_groups=mesh['row'=8,'col'=16] {'row','col'}, use_global_device_ids=true, to_apply=%region_18.19 | all-reduce | flops 1 | bytes 8 | tf_op jit(solution)/shard_map/psum | solution.py:82
  548.3 1.7 multiply_reduce_fusion
  550.0 62.5 %psum.46 = f32[]{:T(128)} all-reduce(f32[]{:T(128)} %get-tuple-element.8), channel_id=1, replica_groups=mesh['row'=8,'col'=16] {'row','col'}, use_global_device_ids=true, to_apply=%region_20.21 | all-reduce | flops 1 | bytes 8 | tf_op jit(solution)/shard_map/psum | solution.py:82
  613.2 0.7 broadcast_divide_fusion
  613.9 0.3 reduce-scatter.8.cloned.1.call-start
  614.2 41.2 %all-gather.8.cloned.1.call-done = f32[8,256,256]{1,2,0:T(8,128)} async-done(((f32[8,256,16]{1,2,0:T(8,128)}), f32[8,256,256]{1,2,0:T(8,128)}) %all-gather.8.cloned.1.call-update) | async-done | bytes 2097168 | tf_op jit(solution)/shard_map/all_gather | solution.py:77
  655.3 6.8 fusion.9
  662.1 5.9 fusion.43
  668.0 73.2 %reduce-scatter.8.cloned.1.call-done = f32[8,256,16]{1,2,0:T(8,128)} async-done(((f32[8,256,256]{1,2,0:T(8,128)}), f32[8,256,16]{1,2,0:T(8,128)}) %reduce-scatter.8.cloned.1.call-update) | async-done | bytes 131088 | tf_op jit(solution)/shard_map/reduce_scatter | solution.py:78
  741.3 1.6 fusion.49
  742.9 65.8 %psum.47 = f32[]{:T(128)} all-reduce(f32[]{:T(128)} %fusion.49), channel_id=1, replica_groups=mesh['row'=8,'col'=16] {'row','col'}, use_global_device_ids=true, to_apply=%region_23.24 | all-reduce | flops 1 | bytes 8 | tf_op jit(solution)/shard_map/psum | solution.py:82
  812.0 0.8 divide_multiply_fusion
  (56 shorter events, 0.6 us)
Async XLA Ops:
  7.2 1.7 copy-start
  21.1 6.4 copy-start.7
  21.1 6.9 copy-start.10
  21.1 7.0 copy-start.11
  21.1 7.1 copy-start.9
  21.1 7.5 copy-start.4
  21.1 8.3 %copy-start.8 = (s32[8,2]{0,1:T(2,128)S(1)}, s32[8,2]{0,1:T(2,128)}, u32[]{:S(2)}) copy-start(s32[8,2]{0,1:T(2,128)} %param.13) | copy-start | bytes 196
  21.1 100.3 %all-to-all-start = ((f32[16,2,256,256]{3,2,1,0:T(8,128)}), f32[16,2,256,256]{3,2,1,0:T(8,128)}, u32[]{:S(2)}, u32[]{:S(2)}) async-start(f32[16,2,256,256]{3,2,1,0:T(8,128)} %select_multiply_fusion), calls=%async_computation | async-start | bytes 16777216 | tf_op jit(solution)/shard_map/all_to_all | solution.py:56
  27.5 100.0 %all-gather.4.cloned.1.call-start = ((), (), s32[]{:S(2)}) async-start(), calls=%async_computation.4 | async-start | bytes 2228224 | tf_op jit(solution)/shard_map/all_gather | solution.py:77
  29.3 184.6 %reduce-scatter.4.cloned.1.call-start = ((), (), s32[]{:S(2)}) async-start(), calls=%async_computation.5 | async-start | bytes 2228224 | tf_op jit(solution)/shard_map/reduce_scatter | solution.py:78
  127.6 6.8 copy-start.1
  140.3 251.4 %all-gather.6.cloned.1.call-start = ((), (), s32[]{:S(2)}) async-start(), calls=%async_computation.6 | async-start | bytes 2228224 | tf_op jit(solution)/shard_map/all_gather | solution.py:77
  350.2 127.4 %reduce-scatter.6.cloned.1.call-start = ((), (), s32[]{:S(2)}) async-start(), calls=%async_computation.7 | async-start | bytes 2228224 | tf_op jit(solution)/shard_map/reduce_scatter | solution.py:78
  391.6 6.8 copy-start.2
  398.4 79.2 %copy-start.5 = (f32[8,256,16]{1,2,0:T(8,128)S(1)}, f32[8,256,16]{1,2,0:T(8,128)}, u32[]{:S(2)}) copy-start(f32[8,256,16]{1,2,0:T(8,128)} %broadcast_divide_fusion.1) | copy-start | bytes 393220
  398.4 149.9 %copy-start.6 = (f32[8,256,16]{1,2,0:T(8,128)S(1)}, f32[8,256,16]{1,2,0:T(8,128)}, u32[]{:S(2)}) copy-start(f32[8,256,16]{1,2,0:T(8,128)} %reduce-scatter.4.cloned.1.call-done) | copy-start | bytes 393220
  404.4 251.0 %all-gather.8.cloned.1.call-start = ((), (), s32[]{:S(2)}) async-start(), calls=%async_computation.8 | async-start | bytes 2228224 | tf_op jit(solution)/shard_map/all_gather | solution.py:77
  613.9 127.4 %reduce-scatter.8.cloned.1.call-start = ((), (), s32[]{:S(2)}) async-start(), calls=%async_computation.9 | async-start | bytes 2228224 | tf_op jit(solution)/shard_map/reduce_scatter | solution.py:78
  655.3 6.8 copy-start.3
Sparse Core Ops, SparseCore 0:
  31.1 46.3 all-gather.3
  140.4 73.5 reduce-scatter.3
  350.3 41.2 all-gather.5
  404.5 73.0 reduce-scatter.5
  614.0 41.2 all-gather.7
  668.2 73.0 reduce-scatter.7
where the time goes:
time: 822 us; the launch traced here: 821 us
  waiting for transfers between devices  390 us (47%)
  blocking collectives  323 us (39%)
  matrix products  38 us (5%)
  between operations  25.5 us (3%)
  other arithmetic  21.1 us (3%)
  local copies, waits for them, and re-layouts  17.1 us (2%)
    psum x5, blocking collectives, combine(): reduced = lax.psum(values, ('row', 'col'))  323 us
    reduce_scatter x3, waiting for transfers between devices, operate(): lax.psum_scatter(contract(full_vector), 'col', scatter_dimension=2, tiled...  220 us
    all_to_all x1, waiting for transfers between devices, local(): lax.all_to_all(outgoing, 'row', split_axis=0, concat_axis=0, tiled=True)  86.8 us
    all_gather x3, waiting for transfers between devices, operate(): full_vector = lax.all_gather(vector, 'col', axis=2, tiled=True)  82.6 us
    dot_general x3, matrix products, contract(): jnp.einsum('swia,sab->swib', left_pick, full_vector, precision=highest)  20.3 us
    dot_general x3, matrix products, contract(): return jnp.einsum('swib,swjb->sij', middle, right_pick, precision=highest)  17.6 us
  transfers between devices with their start and end apart: 7, of which 6 were waited for; matrix products, arithmetic and copies ran while one was open for 2% of the time, Pallas kernels for 0%

commit v1 on v0

--- a/solution.py
+++ b/solution.py
@@ -79,7 +79,7 @@
         return total_sum * start_mask
 
     def combine(values):
-        reduced = lax.psum(values, ("row", "col"))
+        reduced = lax.psum(lax.psum(values, "row"), "col")
         return reduced
 
     image_vec = operate(start_vec)

time: 822 us -> 755 us (0.918)
  blocking collectives: 323 us -> 239 us
  waiting for transfers between devices: 390 us -> 400 us
    psum x5 -> x10, blocking collectives: 323 us -> 239 us  [combine(): reduced = lax.psum(lax.psum(values, 'row'), 'col')]
    all_gather x3, waiting for transfers between devices: 82.6 us -> 92.6 us  [operate(): full_vector = lax.all_gather(vector, 'col', axis=2, tiled=True)]
where the time goes in v1:
time: 755 us; the launch traced here: 747 us
  waiting for transfers between devices  400 us (53%)
  blocking collectives  239 us (32%)
  matrix products  38 us (5%)
  between operations  25.5 us (3%)
  other arithmetic  21.1 us (3%)
  local copies, waits for them, and re-layouts  17.1 us (2%)
    psum x10, blocking collectives, combine(): reduced = lax.psum(lax.psum(values, 'row'), 'col')  239 us
    reduce_scatter x3, waiting for transfers between devices, operate(): lax.psum_scatter(contract(full_vector), 'col', scatter_dimension=2, tiled...  220 us
    all_gather x3, waiting for transfers between devices, operate(): full_vector = lax.all_gather(vector, 'col', axis=2, tiled=True)  92.6 us
    all_to_all x1, waiting for transfers between devices, local(): lax.all_to_all(outgoing, 'row', split_axis=0, concat_axis=0, tiled=True)  86.8 us
    dot_general x3, matrix products, contract(): jnp.einsum('swia,sab->swib', left_pick, full_vector, precision=highest)  20.3 us
    dot_general x3, matrix products, contract(): return jnp.einsum('swib,swjb->sij', middle, right_pick, precision=highest)  17.6 us
  transfers between devices with their start and end apart: 7, of which 6 were waited for; matrix products, arithmetic and copies ran while one was open for 2% of the time, Pallas kernels for 0%

profile of v1, /device:TPU:1, one launch (start us, length us, event | category | flops | bytes accessed | tf_op | source)
XLA Modules:
  0.0 747.1 jit_solution(459190305804180143)
XLA Ops:
  7.2 0.9 eq.29
  8.1 0.2 compare_reduce_fusion
  8.4 0.1 copy.12
  8.5 0.1 reshape.147
  8.7 0.1 copy.14
  8.9 4.3 gather_fusion
  13.2 7.9 %select_multiply_fusion = f32[16,2,256,256]{3,2,1,0:T(8,128)} fusion(f32[16,2,256,256]{3,2,1,0:T(8,128)} %gather_fusion, f32[16]{0:T(128)S(1)} %reshape.149, pred[16]{0:T(512)(128)(4,1)S(1)} %compare_and_fusion.1), kind=kLoop, calls=%fused_computation.3 | loop fusion | flops 4194304 | bytes 16777296 | tf_op jit(solution)/shard_map/mul | solution.py:54
  21.1 6.4 all-to-all-start
  27.6 0.1 fusion.51
  27.8 0.2 reduce_window_sum.19
  28.0 0.2 select_reduce_fusion
  28.2 0.2 select_reduce_fusion.1
  28.6 0.7 multiply_multiply_fusion.3
  29.5 4.9 gather_fusion.2
  34.4 0.1 compare_and_fusion.2
  34.5 86.8 %all-to-all-done = f32[16,2,256,256]{3,2,1,0:T(8,128)} async-done(((f32[16,2,256,256]{3,2,1,0:T(8,128)}), f32[16,2,256,256]{3,2,1,0:T(8,128)}, u32[]{:S(2)}, u32[]{:S(2)}) %all-to-all-start) | async-done | bytes 8388640 | tf_op jit(solution)/shard_map/all_to_all | solution.py:56
  121.4 6.2 gather_fusion.1
  127.6 6.8 fusion.13
  134.4 5.9 fusion.33
  140.3 73.6 %reduce-scatter.4.cloned.1.call-done = f32[8,256,16]{1,2,0:T(8,128)} async-done(((f32[8,256,256]{1,2,0:T(8,128)}), f32[8,256,16]{1,2,0:T(8,128)}) %reduce-scatter.4.cloned.1.call-update) | async-done | bytes 131088 | tf_op jit(solution)/shard_map/reduce_scatter | solution.py:78
  213.9 1.6 multiply_reduce_fusion.4
  215.6 14.7 %all-reduce.1 = (f32[]{:T(128)}, f32[]{:T(128)}) all-reduce(f32[]{:T(128)} %get-tuple-element.3, f32[]{:T(128)} %get-tuple-element.2), channel_id=1, replica_groups=mesh['row'=8,'col'=16] {'row'}, use_global_device_ids=true, to_apply=%region_14.15 | all-reduce | flops 2 | bytes 16 | tf_op jit(solution)/shard_map/psum | solution.py:82
  230.3 31.8 %all-reduce = (f32[]{:T(128)}, f32[]{:T(128)}) all-reduce(f32[]{:T(128)} %get-tuple-element.8, f32[]{:T(128)} %get-tuple-element.9), channel_id=1, replica_groups=mesh['row'=8,'col'=16] {'col'}, use_global_device_ids=true, to_apply=%region_15.16 | all-reduce | flops 2 | bytes 16 | tf_op jit(solution)/shard_map/psum | solution.py:82
  264.1 1.6 multiply_reduce_fusion.2
  265.7 20.5 %psum.88 = f32[]{:T(128)} all-reduce(f32[]{:T(128)} %multiply_reduce_fusion.2), channel_id=1, replica_groups=mesh['row'=8,'col'=16] {'row'}, use_global_device_ids=true, to_apply=%region_17.18 | all-reduce | flops 1 | bytes 8 | tf_op jit(solution)/shard_map/psum | solution.py:82
  286.2 29.1 %psum.89 = f32[]{:T(128)} all-reduce(f32[]{:T(128)} %psum.88), channel_id=1, replica_groups=mesh['row'=8,'col'=16] {'col'}, use_global_device_ids=true, to_apply=%region_18.19 | all-reduce | flops 1 | bytes 8 | tf_op jit(solution)/shard_map/psum | solution.py:82
  316.0 1.7 broadcast_divide_fusion.1
  317.7 0.2 reduce-scatter.6.cloned.1.call-start
  318.0 46.3 %all-gather.6.cloned.1.call-done = f32[8,256,256]{1,2,0:T(8,128)} async-done(((f32[8,256,16]{1,2,0:T(8,128)}), f32[8,256,256]{1,2,0:T(8,128)}) %all-gather.6.cloned.1.call-update) | async-done | bytes 2097168 | tf_op jit(solution)/shard_map/all_gather | solution.py:77
  364.3 6.8 fusion.11
  371.1 5.9 fusion.38
  377.1 73.2 %reduce-scatter.6.cloned.1.call-done = f32[8,256,16]{1,2,0:T(8,128)} async-done(((f32[8,256,256]{1,2,0:T(8,128)}), f32[8,256,16]{1,2,0:T(8,128)}) %reduce-scatter.6.cloned.1.call-update) | async-done | bytes 131088 | tf_op jit(solution)/shard_map/reduce_scatter | solution.py:78
  450.2 1.6 multiply_reduce_fusion.1
  451.9 14.7 %psum.90 = f32[]{:T(128)} all-reduce(f32[]{:T(128)} %multiply_reduce_fusion.1), channel_id=1, replica_groups=mesh['row'=8,'col'=16] {'row'}, use_global_device_ids=true, to_apply=%region_21.22 | all-reduce | flops 1 | bytes 8 | tf_op jit(solution)/shard_map/psum | solution.py:82
  466.5 31.8 %psum.91 = f32[]{:T(128)} all-reduce(f32[]{:T(128)} %psum.90), channel_id=1, replica_groups=mesh['row'=8,'col'=16] {'col'}, use_global_device_ids=true, to_apply=%region_22.23 | all-reduce | flops 1 | bytes 8 | tf_op jit(solution)/shard_map/psum | solution.py:82
  501.7 1.7 multiply_reduce_fusion
  503.4 20.5 %psum.92 = f32[]{:T(128)} all-reduce(f32[]{:T(128)} %get-tuple-element.10), channel_id=1, replica_groups=mesh['row'=8,'col'=16] {'row'}, use_global_device_ids=true, to_apply=%region_24.25 | all-reduce | flops 1 | bytes 8 | tf_op jit(solution)/shard_map/psum | solution.py:82
  523.9 29.2 %psum.93 = f32[]{:T(128)} all-reduce(f32[]{:T(128)} %psum.92), channel_id=1, replica_groups=mesh['row'=8,'col'=16] {'col'}, use_global_device_ids=true, to_apply=%region_25.26 | all-reduce | flops 1 | bytes 8 | tf_op jit(solution)/shard_map/psum | solution.py:82
  553.8 0.7 broadcast_divide_fusion
  554.4 0.3 reduce-scatter.8.cloned.1.call-start
  554.7 46.3 %all-gather.8.cloned.1.call-done = f32[8,256,256]{1,2,0:T(8,128)} async-done(((f32[8,256,16]{1,2,0:T(8,128)}), f32[8,256,256]{1,2,0:T(8,128)}) %all-gather.8.cloned.1.call-update) | async-done | bytes 2097168 | tf_op jit(solution)/shard_map/all_gather | solution.py:77
  601.0 6.8 fusion.9
  607.8 5.9 fusion.43
  613.7 73.2 %reduce-scatter.8.cloned.1.call-done = f32[8,256,16]{1,2,0:T(8,128)} async-done(((f32[8,256,256]{1,2,0:T(8,128)}), f32[8,256,16]{1,2,0:T(8,128)}) %reduce-scatter.8.cloned.1.call-update) | async-done | bytes 131088 | tf_op jit(solution)/shard_map/reduce_scatter | solution.py:78
  686.9 1.6 fusion.49
  688.5 14.7 %psum.94 = f32[]{:T(128)} all-reduce(f32[]{:T(128)} %fusion.49), channel_id=1, replica_groups=mesh['row'=8,'col'=16] {'row'}, use_global_device_ids=true, to_apply=%region_28.29 | all-reduce | flops 1 | bytes 8 | tf_op jit(solution)/shard_map/psum | solution.py:82
  703.2 31.8 %psum.95 = f32[]{:T(128)} all-reduce(f32[]{:T(128)} %psum.94), channel_id=1, replica_groups=mesh['row'=8,'col'=16] {'col'}, use_global_device_ids=true, to_apply=%region_29.30 | all-reduce | flops 1 | bytes 8 | tf_op jit(solution)/shard_map/psum | solution.py:82
  738.3 0.8 divide_multiply_fusion
  (61 shorter events, 1.1 us)
Async XLA Ops:
  7.2 1.7 copy-start
  21.1 6.4 copy-start.7
  21.1 6.9 copy-start.10
  21.1 7.0 copy-start.11
  21.1 7.1 copy-start.9
  21.1 7.5 %copy-start.4 = (f32[8,256,16]{1,2,0:T(8,128)S(1)}, f32[8,256,16]{1,2,0:T(8,128)}, u32[]{:S(2)}) copy-start(f32[8,256,16]{1,2,0:T(8,128)} %param.8) | copy-start | bytes 393220
  21.1 8.3 %copy-start.8 = (s32[8,2]{0,1:T(2,128)S(1)}, s32[8,2]{0,1:T(2,128)}, u32[]{:S(2)}) copy-start(s32[8,2]{0,1:T(2,128)} %param.13) | copy-start | bytes 196
  21.1 100.3 %all-to-all-start = ((f32[16,2,256,256]{3,2,1,0:T(8,128)}), f32[16,2,256,256]{3,2,1,0:T(8,128)}, u32[]{:S(2)}, u32[]{:S(2)}) async-start(f32[16,2,256,256]{3,2,1,0:T(8,128)} %select_multiply_fusion), calls=%async_computation | async-start | bytes 16777216 | tf_op jit(solution)/shard_map/all_to_all | solution.py:56
  27.5 100.0 %all-gather.4.cloned.1.call-start = ((), (), s32[]{:S(2)}) async-start(), calls=%async_computation.4 | async-start | bytes 2228224 | tf_op jit(solution)/shard_map/all_gather | solution.py:77
  29.3 184.6 %reduce-scatter.4.cloned.1.call-start = ((), (), s32[]{:S(2)}) async-start(), calls=%async_computation.5 | async-start | bytes 2228224 | tf_op jit(solution)/shard_map/reduce_scatter | solution.py:78
  127.6 6.8 copy-start.1
  140.3 224.0 %all-gather.6.cloned.1.call-start = ((), (), s32[]{:S(2)}) async-start(), calls=%async_computation.6 | async-start | bytes 2228224 | tf_op jit(solution)/shard_map/all_gather | solution.py:77
  317.7 132.5 %reduce-scatter.6.cloned.1.call-start = ((), (), s32[]{:S(2)}) async-start(), calls=%async_computation.7 | async-start | bytes 2228224 | tf_op jit(solution)/shard_map/reduce_scatter | solution.py:78
  364.3 6.8 copy-start.2
  371.1 79.2 %copy-start.5 = (f32[8,256,16]{1,2,0:T(8,128)S(1)}, f32[8,256,16]{1,2,0:T(8,128)}, u32[]{:S(2)}) copy-start(f32[8,256,16]{1,2,0:T(8,128)} %broadcast_divide_fusion.1) | copy-start | bytes 393220
  371.1 130.6 %copy-start.6 = (f32[8,256,16]{1,2,0:T(8,128)S(1)}, f32[8,256,16]{1,2,0:T(8,128)}, u32[]{:S(2)}) copy-start(f32[8,256,16]{1,2,0:T(8,128)} %reduce-scatter.4.cloned.1.call-done) | copy-start | bytes 393220
  377.0 224.0 %all-gather.8.cloned.1.call-start = ((), (), s32[]{:S(2)}) async-start(), calls=%async_computation.8 | async-start | bytes 2228224 | tf_op jit(solution)/shard_map/all_gather | solution.py:77
  554.4 132.5 %reduce-scatter.8.cloned.1.call-start = ((), (), s32[]{:S(2)}) async-start(), calls=%async_computation.9 | async-start | bytes 2228224 | tf_op jit(solution)/shard_map/reduce_scatter | solution.py:78
  601.0 6.8 copy-start.3
Sparse Core Ops, SparseCore 0:
  31.1 46.3 all-gather.3
  140.4 73.5 reduce-scatter.3
  317.9 46.3 all-gather.5
  377.1 73.0 reduce-scatter.5
  554.6 46.3 all-gather.7
  613.8 73.0 reduce-scatter.7
